TPU v7x, 32 devices: a whole 2x2x4 slice. The times are simulated.
32 devices in a mesh: groups: 2 (over x), mp: 8 (over z, y), row: 2 (over core).
Axes of the slice: x: 2, y: 2, z: 4, core: 2. Of those that a mesh axis runs over, the one named last changes fastest.
Arguments:
- stream: bfloat16 [2, 256, 4096], P(None, ('groups', 'row'), 'mp'), parts along dimension 1, may hold values from -12 to 12
- projected: bfloat16 [2, 256, 2, 8192], P(None, ('groups', 'row'), None, 'mp'), parts along dimension 1, may hold values from -6 to 6
- conv_state: bfloat16 [256, 3, 8192], P(('groups', 'row'), None, 'mp'), parts along dimension 0, may hold values from -6 to 6
- scan_state: float32 [256, 16, 8192], P(('groups', 'row'), None, 'mp'), parts along dimension 0, may hold values from -6 to 6
- conv_weight: float32 [4, 8192], P(None, 'mp'), may hold values from -3 to 3
- conv_bias: float32 [8192], P('mp'), may hold values from -3 to 3
- state_proj: bfloat16 [8192, 288], P('mp'), may hold values from -0.0625 to 0.0625
- step_proj: bfloat16 [256, 8192], P(None, 'mp'), may hold values from -0.375 to 0.375
- step_bias: float32 [8192], P('mp'), may hold values from -3 to 0.5
- decay_log: float32 [16, 8192], P(None, 'mp'), may hold values from -4 to 2
- skip_gain: float32 [8192], P('mp'), may hold values from 0.25 to 1.75
- out_weight: bfloat16 [8192, 4096], P('mp'), may hold values from -0.09375 to 0.09375
- norm_gain: float32 [4096], replicated, may hold values from 0.25 to 1.75
- router: bfloat16 [16, 4096], replicated, may hold values from -0.09375 to 0.09375
- expert_gate: bfloat16 [2, 4096, 12288], P('row', None, 'mp'), may hold values from -0.09375 to 0.09375
- expert_up: bfloat16 [2, 4096, 12288], P('row', None, 'mp'), may hold values from -0.09375 to 0.09375
- expert_down: bfloat16 [2, 12288, 4096], P('row', 'mp'), may hold values from -0.078125 to 0.078125
- expert_ids: int32 [2, 256, 2], P(None, ('groups', 'row')), parts along dimension 1, may hold values from 0 to 15, as said below
Outputs:
- mixed_out: bfloat16 [2, 256, 4096], P(None, ('groups', 'row'), 'mp'), parts along dimension 1
- new_state: float32 [256, 16, 8192], P(('groups', 'row'), None, 'mp'), parts along dimension 0
There are 2 independent parts, one for each index of `groups`. A program takes and returns all parts, laid end to end along the dimension named above; an argument that names none is the same for every part. Nothing has to cross between parts.
Inputs may be any that keep to these rules, and one draw needn't show every extreme that they name: `expert_ids`: A row's two ids differ. In each step, at most 16 of the rows of one device (aligned blocks of 64 rows) choose expert 0, and at most 16 choose expert 1; in every draw some step has exactly 16 such rows for both experts in every block.
All inputs are finite; a program needn't handle non-finite values.
Results may differ from a plain program's by a relative error of at most 0.006.
Values may be sent and summed in bfloat16 or wider, within the bound.
A program may use at most 128 MiB of HBM per device.

v0:
```python
import jax
import jax.numpy as jnp
from jax import lax
from jax.sharding import PartitionSpec as P

CAP = 16


def expert_apply(tokens_in, gate_weight, up_weight, down_weight):
    gate_part = jnp.dot(tokens_in, gate_weight, preferred_element_type=jnp.float32)
    up_part = jnp.dot(tokens_in, up_weight, preferred_element_type=jnp.float32)
    hidden = (jax.nn.silu(gate_part) * up_part).astype(jnp.bfloat16)
    return jnp.dot(hidden, down_weight, preferred_element_type=jnp.float32)


def on_device(
    stream,
    projected,
    conv_state,
    scan_state,
    conv_weight,
    conv_bias,
    state_proj,
    step_proj,
    step_bias,
    decay_log,
    skip_gain,
    out_weight,
    norm_gain,
    router,
    expert_gate,
    expert_up,
    expert_down,
    expert_ids,
):
    step_count, row_count, width_local = stream.shape
    inner_local = projected.shape[3]
    kernel_size = conv_weight.shape[0]
    rank_size = step_proj.shape[0]
    state_size = decay_log.shape[0]
    full_width = out_weight.shape[1]
    flat_rows = step_count * row_count
    inputs = projected[:, :, 0, :]
    gate_side = projected[:, :, 1, :]
    history = jnp.concatenate(
        [conv_state.astype(jnp.float32), jnp.transpose(inputs, (1, 0, 2)).astype(jnp.float32)],
        axis=1,
    )
    conv_list = []
    for step_no in range(step_count):
        window = history[:, step_no : step_no + kernel_size, :]
        conv_list.append(
            jax.nn.silu(jnp.sum(window * conv_weight[None], axis=1) + conv_bias).astype(
                jnp.bfloat16
            )
        )
    convolved = jnp.stack(conv_list)
    local_proj = jnp.dot(
        convolved.reshape(flat_rows, inner_local), state_proj, preferred_element_type=jnp.float32
    )
    projections = lax.psum(local_proj, "mp").reshape(step_count, row_count, -1)
    low_rank = projections[..., :rank_size].astype(jnp.bfloat16)
    input_gain = projections[..., rank_size : rank_size + state_size]
    output_gain = projections[..., rank_size + state_size :]
    timestep = jax.nn.softplus(
        jnp.dot(
            low_rank.reshape(flat_rows, rank_size), step_proj, preferred_element_type=jnp.float32
        ).reshape(step_count, row_count, inner_local)
        + step_bias
    )
    decay_rates = jnp.exp(decay_log)
    carried = scan_state
    outputs = []
    for step_no in range(step_count):
        current = convolved[step_no].astype(jnp.float32)
        delta_now = timestep[step_no]
        decay_now = jnp.exp(-delta_now[:, None, :] * decay_rates[None])
        carried = (
            decay_now * carried
            + (delta_now * current)[:, None, :] * input_gain[step_no][:, :, None]
        )
        readout = jnp.sum(output_gain[step_no][:, :, None] * carried, axis=1) + skip_gain * current
        outputs.append(
            (readout * jax.nn.silu(gate_side[step_no].astype(jnp.float32))).astype(jnp.bfloat16)
        )
    scanned = jnp.stack(outputs).reshape(flat_rows, inner_local)
    partial_value = jnp.dot(scanned, out_weight, preferred_element_type=jnp.float32)
    offset = lax.axis_index("mp") * width_local
    own_part = stream.reshape(flat_rows, width_local).astype(jnp.float32)
    placed = lax.dynamic_update_slice_in_dim(
        partial_value,
        lax.dynamic_slice_in_dim(partial_value, offset, width_local, 1) + own_part,
        offset,
        1,
    )
    after_full = lax.psum(placed, "mp").astype(jnp.bfloat16)
    after_own = lax.dynamic_slice_in_dim(after_full, offset, width_local, 1)
    widened = after_full.astype(jnp.float32)
    normed = (
        widened * lax.rsqrt(jnp.mean(widened * widened, axis=-1, keepdims=True) + 1e-05) * norm_gain
    ).astype(jnp.bfloat16)
    logits = lax.dot_general(
        normed, router, (((1,), (1,)), ((), ())), preferred_element_type=jnp.float32
    )
    picked = expert_ids.reshape(flat_rows, -1)
    expert_total = router.shape[0]
    onehot = picked[:, :, None] == jnp.arange(expert_total)[None, None, :]
    chosen = jnp.sum(jnp.where(onehot, logits[:, None, :], 0.0), axis=2)
    weights = jnp.exp(chosen)
    shares = weights / jnp.sum(weights, axis=1, keepdims=True)
    in_flight = lax.axis_size("row")
    weight_rows = jnp.stack(
        [jnp.sum(jnp.where(picked == expert, shares, 0.0), axis=1) for expert in range(in_flight)],
        axis=1,
    )
    gate_weight = expert_gate[0]
    up_weight = expert_up[0]
    down_weight = expert_down[0]
    routed = jnp.any(picked[:, None, :] == jnp.arange(in_flight)[None, :, None], axis=2)
    position = (
        jnp.cumsum(routed.reshape(step_count, row_count, in_flight).astype(jnp.int32), axis=1) - 1
    ).reshape(flat_rows, in_flight)
    slot_total = step_count * CAP
    slot_index = jnp.arange(slot_total)
    row_step = jnp.arange(flat_rows) // row_count
    matching = (
        jnp.transpose(routed)[:, None, :]
        & (row_step[None, None, :] == (slot_index // CAP)[None, :, None])
        & (jnp.transpose(position)[:, None, :] == (slot_index % CAP)[None, :, None])
    )
    select_half = matching.astype(jnp.bfloat16)
    select_full = matching.astype(jnp.float32)
    outgoing = jnp.einsum(
        "esm,mx->esx", select_half, normed, preferred_element_type=jnp.float32
    ).astype(jnp.bfloat16)
    slot_share = jnp.einsum("esm,me->es", select_full, weight_rows, precision=lax.Precision.HIGHEST)
    arrived = lax.all_to_all(outgoing, "row", split_axis=0, concat_axis=0, tiled=True)
    count_here = arrived.shape[1]
    produced = expert_apply(
        arrived.reshape(-1, full_width), gate_weight, up_weight, down_weight
    ).reshape(in_flight, count_here, full_width)
    returned = lax.all_to_all(
        produced.astype(jnp.bfloat16), "row", split_axis=0, concat_axis=0, tiled=True
    ).astype(produced.dtype)
    combined = jnp.einsum(
        "esm,esx->mx",
        select_full,
        returned * slot_share[:, :, None],
        precision=lax.Precision.HIGHEST,
    )
    combined = lax.psum_scatter(combined, "mp", scatter_dimension=1, tiled=True)
    mixed_out = (
        (after_own.astype(jnp.float32) + combined)
        .astype(jnp.bfloat16)
        .reshape(step_count, row_count, width_local)
    )
    return (mixed_out, carried)


def solution(mesh):
    return jax.shard_map(
        on_device,
        mesh=mesh,
        in_specs=(
            P(None, ("groups", "row"), "mp"),
            P(None, ("groups", "row"), None, "mp"),
            P(("groups", "row"), None, "mp"),
            P(("groups", "row"), None, "mp"),
            P(None, "mp"),
            P("mp"),
            P("mp", None),
            P(None, "mp"),
            P("mp"),
            P(None, "mp"),
            P("mp"),
            P("mp", None),
            P(),
            P(),
            P("row", None, "mp"),
            P("row", None, "mp"),
            P("row", "mp", None),
            P(None, ("groups", "row"), None),
        ),
        out_specs=(P(None, ("groups", "row"), "mp"), P(("groups", "row"), None, "mp")),
        check_vma=False,
    )
```

profile of v0, /device:TPU:0, one launch (start us, length us, event | category | flops | bytes accessed | tf_op | source)
XLA Modules:
  0.0 296.4 jit_solution(5089809884289274848)
XLA Ops:
  7.2 0.0 copy-start
  7.2 0.0 copy-start.2
  7.2 0.0 copy-start.5
  7.2 0.0 all-reduce.3.cloned.1.call-start
  7.2 1.2 copy.64
  8.5 0.0 copy-start.6
  8.5 0.0 copy-start.4
  8.5 0.0 copy-start.8
  8.5 0.0 copy-start.11
  8.5 1.1 maximum_convert_fusion
  9.6 0.9 fusion.19
  10.6 0.0 copy-done.5
  10.6 0.2 multiply_convert_fusion.3
  10.8 0.0 copy-done
  10.8 1.1 fusion.59
  11.9 0.0 all-reduce.3.cloned.1.call-update
  11.9 0.0 reduce-scatter.2.cloned.1.call-start
  12.0 0.0 copy-done.2
  12.0 0.6 fusion.58
  12.6 0.0 copy-done.6
  12.6 0.1 eq.75
  12.7 0.1 copy.51
  12.8 0.1 reduce_window_sum.11
  12.9 0.1 copy.45
  13.0 0.0 copy-done.4
  13.0 0.1 broadcast_compare_fusion
  13.1 72.3 %all-reduce.3.cloned.1.call-done = f32[2,64,288]{2,1,0:T(8,128)} async-done(((f32[2,64,288]{2,1,0:T(8,128)}), f32[2,64,288]{2,1,0:T(8,128)}) %all-reduce.3.cloned.1.call-update) | async-done | bytes 147472 | tf_op jit(solution)/shard_map/psum | solution.py:61
  85.4 0.0 copy-done.8
  85.4 0.0 copy-done.11
  85.4 1.5 compare_select_fusion
  87.0 0.2 convert_multiply_fusion.5
  87.1 0.9 slice_bitcast_fusion.5
  88.1 0.0 copy-start.7
  88.1 0.0 slice-start.4
  88.1 7.0 %multiply_reduce_fusion = (f32[64,1024]{1,0:T(8,128)S(1)}, f32[64,16,1024]{2,1,0:T(8,128)}, f32[64,1024]{1,0:T(8,128)S(1)}) fusion(f32[64,16]{1,0:T(8,128)S(1)} %get-tuple-element.17, f32[64,16]{1,0:T(8,128)S(1)} %get-tuple-element.16, f32[64,1024]{1,0:T(8,128)S(1)} %get-tuple-element.10, f32[64,16]{1,0:T(8,128)S(1)} %get-tuple-element.18, ...), kind=kLoop, calls=%fused_computation.9 | loop fusion | flops 12451840 | bytes 10043392 | tf_op jit(solution)/shard_map/reduce_sum | solution.py:82
  95.1 0.0 copy-done.7
  95.1 0.2 fusion.40
  95.3 0.0 copy-start.3
  95.4 1.3 fusion.60
  96.7 0.0 copy-start.9
  96.7 0.0 copy-start.10
  96.7 92.4 %all-reduce.4 = bf16[128,4096]{1,0:T(8,128)(2,1)} all-reduce(f32[128,4096]{1,0:T(8,128)S(1)} %fusion.38), channel_id=1, replica_groups=mesh['groups'=2,'mp'=8,'row'=2] {'mp'}, use_global_device_ids=true, to_apply=%region_5.6 | all-reduce | flops 524288 | bytes 3145728 | tf_op jit(solution)/shard_map/psum | solution.py:96
  189.1 1.5 fusion.15
  190.7 1.7 fusion.27
  192.4 0.1 div.112
  192.5 0.1 exp.98
  192.6 0.1 stack.21
  192.7 0.1 stack.22
  192.8 0.0 slice-start
  192.8 1.9 convolution_convert_fusion
  194.7 0.2 fusion.43
  194.9 4.2 %all_to_all.10 = bf16[2,32,4096]{2,1,0:T(8,128)(2,1)S(1)} all-to-all(bf16[2,32,4096]{2,1,0:T(8,128)(2,1)S(1)} %convolution_convert_fusion), channel_id=1, replica_groups=mesh['groups'=2,'mp'=8,'row'=2] {'row'}, dimensions={0} | all-to-all | bytes 1048576 | tf_op jit(solution)/shard_map/all_to_all | solution.py:137
  199.1 7.0 %fusion.4 = f32[64,1536]{1,0:T(8,128)S(1)} fusion(bf16[64,4096]{1,0:T(8,128)(2,1)S(1)} %bitcast.119, bf16[1,4096,1536]{2,1,0:T(8,128)(2,1)} %param.32), kind=kOutput, calls=%fused_computation.4 | convolution fusion | flops 805306368 | bytes 13500416 | tf_op jit(solution)/shard_map/dot_general | solution.py:10
  206.0 0.0 slice-done
  206.0 0.0 slice-done.2
  206.1 2.3 fusion.12
  208.4 0.1 slice-done.6
  208.5 1.4 slice-done.7
  209.9 2.3 fusion.6
  212.2 4.2 %all_to_all.11 = bf16[2,32,4096]{2,1,0:T(8,128)(2,1)S(1)} all-to-all(bf16[2,32,4096]{2,1,0:T(8,128)(2,1)S(1)} %fusion.6), channel_id=1, replica_groups=mesh['groups'=2,'mp'=8,'row'=2] {'row'}, dimensions={0} | all-to-all | bytes 1048576 | tf_op jit(solution)/shard_map/all_to_all | solution.py:142
  216.4 2.4 convolution_bitcast_fusion
  218.8 0.0 reduce-scatter.2.cloned.1.call-update
  218.8 69.1 %reduce-scatter.2.cloned.1.call-done = f32[128,512]{1,0:T(8,128)} async-done(((f32[128,4096]{1,0:T(8,128)}), f32[128,512]{1,0:T(8,128)}) %reduce-scatter.2.cloned.1.call-update) | async-done | bytes 262160 | tf_op jit(solution)/shard_map/reduce_scatter | solution.py:151
  287.9 1.7 add_convert_fusion
  (33 shorter events, 0.3 us)
Async XLA Ops:
  7.2 3.6 %copy-start = (bf16[1024,288]{0,1:T(8,128)(2,1)S(1)}, bf16[1024,288]{0,1:T(8,128)(2,1)}, u32[]{:S(2)}) copy-start(bf16[1024,288]{0,1:T(8,128)(2,1)} %param.24) | copy-start | bytes 1769476
  7.2 4.8 %copy-start.2 = (bf16[2,64,2,1024]{3,2,1,0:T(2,128)(2,1)S(1)}, bf16[2,64,2,1024]{3,2,1,0:T(2,128)(2,1)}, u32[]{:S(2)}) copy-start(bf16[2,64,2,1024]{3,2,1,0:T(2,128)(2,1)} %param.19) | copy-start | bytes 1572868
  7.2 3.4 %copy-start.5 = (f32[1024]{0:T(1024)S(1)}, f32[1024]{0:T(1024)}, u32[]{:S(2)}) copy-start(f32[1024]{0:T(1024)} %param.23) | copy-start | bytes 12292
  7.2 78.2 %all-reduce.3.cloned.1.call-start = ((), (), s32[]{:S(2)}) async-start(), calls=%async_computation.3 | async-start | bytes 393216 | tf_op jit(solution)/shard_map/psum | solution.py:61
  8.5 4.1 %copy-start.6 = (s32[2,64,2]{1,2,0:T(2,128)S(1)}, s32[2,64,2]{1,2,0:T(2,128)}, u32[]{:S(2)}) copy-start(s32[2,64,2]{1,2,0:T(2,128)} %param.35) | copy-start | bytes 3076
  8.5 4.5 %copy-start.4 = (f32[16,1024]{1,0:T(8,128)S(1)}, f32[16,1024]{1,0:T(8,128)}, u32[]{:S(2)}) copy-start(f32[16,1024]{1,0:T(8,128)} %param.27) | copy-start | bytes 196612
  8.5 77.0 %copy-start.8 = (bf16[256,1024]{1,0:T(8,128)(2,1)S(1)}, bf16[256,1024]{1,0:T(8,128)(2,1)}, u32[]{:S(2)}) copy-start(bf16[256,1024]{1,0:T(8,128)(2,1)} %param.25) | copy-start | bytes 1572868
  8.5 76.9 %copy-start.11 = (f32[1024]{0:T(1024)S(1)}, f32[1024]{0:T(1024)}, u32[]{:S(2)}) copy-start(f32[1024]{0:T(1024)} %param.26) | copy-start | bytes 12292
  11.9 276.0 %reduce-scatter.2.cloned.1.call-start = ((), (), s32[]{:S(2)}) async-start(), calls=%async_computation.4 | async-start | bytes 2359296 | tf_op jit(solution)/shard_map/reduce_scatter | solution.py:151
  85.4 9.9 %slice-start.3 = ((s8[8388608]{0:T(1024)(128)(4,1)}), s8[4194304]{0:T(1024)(128)(4,1)S(1)}, s32[]{:S(2)}) async-start(s8[8388608]{0:T(1024)(128)(4,1)} %bitcast.115), calls=%async_computation.8 | async-start | bytes 8388608
  88.1 7.0 %copy-start.7 = (f32[1024]{0:T(1024)S(1)}, f32[1024]{0:T(1024)}, u32[]{:S(2)}) copy-start(f32[1024]{0:T(1024)} %param.28) | copy-start | bytes 12292
  88.1 7.3 %slice-start.4 = ((s8[8388608]{0:T(1024)(128)(4,1)}), s8[4194304]{0:T(1024)(128)(4,1)S(1)}, s32[]{:S(2)}) async-start(s8[8388608]{0:T(1024)(128)(4,1)} %bitcast.115), calls=%async_computation.9 | async-start | bytes 8388608
  95.3 1.3 copy-start.3
  96.7 94.0 %copy-start.9 = (bf16[16,4096]{1,0:T(8,128)(2,1)S(1)}, bf16[16,4096]{1,0:T(8,128)(2,1)}, u32[]{:S(2)}) copy-start(bf16[16,4096]{1,0:T(8,128)(2,1)} %param.31) | copy-start | bytes 393220
  96.7 94.0 %copy-start.10 = (f32[4096]{0:T(1024)S(1)}, f32[4096]{0:T(1024)}, u32[]{:S(2)}) copy-start(f32[4096]{0:T(1024)} %param.30) | copy-start | bytes 49156
  192.8 13.3 %slice-start = ((s8[12582912]{0:T(1024)(128)(4,1)}), s8[4194304]{0:T(1024)(128)(4,1)S(1)}, s32[]{:S(2)}) async-start(s8[12582912]{0:T(1024)(128)(4,1)} %bitcast.113), calls=%async_computation.5 | async-start | bytes 8388608
  199.0 7.0 %slice-start.1 = ((s8[12582912]{0:T(1024)(128)(4,1)}), s8[4194304]{0:T(1024)(128)(4,1)S(1)}, s32[]{:S(2)}) async-start(s8[12582912]{0:T(1024)(128)(4,1)} %bitcast.113), calls=%async_computation.6 | async-start | bytes 8388608
  199.1 7.0 %slice-start.2 = ((s8[12582912]{0:T(1024)(128)(4,1)}), s8[4194304]{0:T(1024)(128)(4,1)S(1)}, s32[]{:S(2)}) async-start(s8[12582912]{0:T(1024)(128)(4,1)} %bitcast.113), calls=%async_computation.7 | async-start | bytes 8388608
  199.1 9.3 %slice-start.5 = ((s8[12582912]{0:T(1024)(128)(4,1)}), s8[4194304]{0:T(1024)(128)(4,1)S(1)}, s32[]{:S(2)}) async-start(s8[12582912]{0:T(1024)(128)(4,1)} %bitcast.117), calls=%async_computation.10 | async-start | bytes 8388608
  199.1 9.4 %slice-start.6 = ((s8[12582912]{0:T(1024)(128)(4,1)}), s8[4194304]{0:T(1024)(128)(4,1)S(1)}, s32[]{:S(2)}) async-start(s8[12582912]{0:T(1024)(128)(4,1)} %bitcast.117), calls=%async_computation.11 | async-start | bytes 8388608
  206.1 3.8 %slice-start.7 = ((s8[12582912]{0:T(1024)(128)(4,1)}), s8[4194304]{0:T(1024)(128)(4,1)S(1)}, s32[]{:S(2)}) async-start(s8[12582912]{0:T(1024)(128)(4,1)} %bitcast.117), calls=%async_computation.12 | async-start | bytes 8388608
  209.9 79.7 %copy-start.1 = (bf16[1024,288]{0,1:T(8,128)(2,1)S(1)}, bf16[1024,288]{0,1:T(8,128)(2,1)}, u32[]{:S(2)}) copy-start(bf16[1024,288]{0,1:T(8,128)(2,1)} %param.24) | copy-start | bytes 1769476
Sparse Core Ops, SparseCore 0:
  12.0 73.3 all-reduce.2
  218.9 68.9 reduce-scatter.1
where the time goes:
time: 297 us; the launch traced here: 296 us
  waiting for transfers between devices  141 us (47%)
  blocking collectives  101 us (34%)
  matrix products  21.6 us (7%)
  between operations  14.4 us (5%)
  other arithmetic  13.2 us (4%)
  local copies, waits for them, and re-layouts  4.98 us (2%)
    psum x1, blocking collectives, on_device(): after_full = lax.psum(placed, 'mp').astype(jnp.bfloat16)  92.4 us
    psum x1, waiting for transfers between devices, on_device(): projections = lax.psum(local_proj, 'mp').reshape(step_count, row_count, -1)  72.3 us
    reduce_scatter x1, waiting for transfers between devices, on_device(): combined = lax.psum_scatter(combined, 'mp', scatter_dimension=1, tiled=True)  69.1 us
    reduce_sum x1, other arithmetic, on_device(): jnp.sum(output_gain[step_no][:, :, None] * carried, axis=1)  6.97 us
    dot_general x1, matrix products, expert_apply(): jnp.dot(tokens_in, gate_weight, preferred_element_type=jnp.float32)  6.97 us
  transfers between devices with their start and end apart: 2, of which 2 were waited for; matrix products, arithmetic and copies ran while one was open for 0% of the time, Pallas kernels for 0%

commit v1 on v0

v1 whole, which is shorter than its diff:
```python
import functools

import jax
import jax.numpy as jnp
from jax import lax
from jax.experimental import pallas as pl
from jax.experimental.pallas import tpu as pltpu
from jax.sharding import PartitionSpec as P

CAP = 16
MESH = pl.DeviceIdType.MESH
F32 = jnp.float32
BF16 = jnp.bfloat16


def far_first(n):
    return sorted(range(1, n), key=lambda off: -min(off, n - off))


def sum_kernel(n, x_ref, o_ref, recv, own, send_a, recv_a, send_b, recv_b):
    me = lax.axis_index("mp")
    barrier = pltpu.get_barrier_semaphore()
    for off in range(1, n):
        pl.semaphore_signal(
            barrier, inc=1, device_id={"mp": lax.rem(me + off, n)}, device_id_type=MESH
        )
    pl.semaphore_wait(barrier, n - 1)
    order = far_first(n)
    first = {}
    for off in order:
        to = lax.rem(me + off, n)
        first[off] = pltpu.make_async_remote_copy(
            src_ref=x_ref.at[to],
            dst_ref=recv.at[off],
            send_sem=send_a.at[off],
            recv_sem=recv_a.at[off],
            device_id={"mp": to},
            device_id_type=MESH,
        )
        first[off].start()
    total = x_ref[me].astype(F32)
    for off in reversed(order):
        first[off].wait_recv()
        total = total + recv[off].astype(F32)
    own[...] = total.astype(own.dtype)
    second = {}
    for off in order:
        to = lax.rem(me + off, n)
        second[off] = pltpu.make_async_remote_copy(
            src_ref=own,
            dst_ref=o_ref.at[me],
            send_sem=send_b.at[off],
            recv_sem=recv_b.at[off],
            device_id={"mp": to},
            device_id_type=MESH,
        )
        second[off].start()
    o_ref[me] = own[...]
    for off in order:
        first[off].wait_send()
        second[off].wait()


def sum_over_mp(n, value):
    rows, cols = value.shape
    part = (rows // n, cols)
    dma = pltpu.SemaphoreType.DMA((n,))
    out = pl.pallas_call(
        functools.partial(sum_kernel, n),
        out_shape=jax.ShapeDtypeStruct((n,) + part, BF16),
        in_specs=[pl.BlockSpec(memory_space=pltpu.VMEM)],
        out_specs=pl.BlockSpec(memory_space=pltpu.VMEM),
        scratch_shapes=[
            pltpu.VMEM((n,) + part, BF16),
            pltpu.VMEM(part, BF16),
            dma,
            dma,
            dma,
            dma,
        ],
        compiler_params=pltpu.CompilerParams(collective_id=0, has_side_effects=True),
        name="sum_over_mp",
    )(value.astype(BF16).reshape((n,) + part))
    return out.reshape(rows, cols)


def tail_kernel(
    n,
    row_size,
    steps,
    tile,
    scanned,
    stream,
    gain,
    router,
    picked,
    picked_t,
    out_hbm,
    gate_hbm,
    up_hbm,
    down_hbm,
    o_ref,
    out_weight,
    gate,
    up,
    down,
    send1,
    recv1,
    stage,
    gathered,
    id_stage,
    ids,
    normed,
    hidden,
    send2,
    recv2,
    load_sem,
    s1,
    r1,
    s2,
    r2,
    si,
    ri,
    s3,
    r3,
):
    me = lax.axis_index("mp")
    row = lax.axis_index("row")
    flat, width = stream.shape
    full = normed.shape[1]
    slots = steps * CAP
    per_step = flat // steps
    peers = [(a, b) for b in [0] + far_first(n) for a in range(row_size) if a or b]

    def at(a, b):
        return {"row": lax.rem(row + a, row_size), "mp": lax.rem(me + b, n)}

    def cols(index):
        return pl.ds(pl.multiple_of(index * width, width), width)

    loads = [
        pltpu.make_async_copy(src, dst, load_sem.at[k])
        for k, (src, dst) in enumerate(
            [
                (out_hbm, out_weight),
                (gate_hbm.at[0], gate),
                (up_hbm.at[0], up),
                (down_hbm.at[0], down),
            ]
        )
    ]
    for load in loads:
        load.start()
    barrier = pltpu.get_barrier_semaphore()
    for a, b in peers:
        pl.semaphore_signal(barrier, inc=1, device_id=at(a, b), device_id_type=MESH)

    def iota(shape, dim):
        return lax.broadcasted_iota(jnp.int32, shape, dim)

    same_step = (iota((flat, flat), 0) // per_step) == (iota((flat, flat), 1) // per_step)
    lower = (same_step & (iota((flat, flat), 1) <= iota((flat, flat), 0))).astype(F32).astype(BF16)
    upper = (same_step & (iota((flat, flat), 0) <= iota((flat, flat), 1))).astype(F32).astype(BF16)
    choice = picked[...]
    choice_t = picked_t[...]
    top = choice.shape[1]
    select, spread = [], []
    for expert in range(row_size):
        hit_t = jnp.zeros((1, flat), F32)
        hit = jnp.zeros((flat, 1), F32)
        for k in range(top):
            hit_t = hit_t + (choice_t[k : k + 1, :] == expert).astype(F32)
            hit = hit + (choice[:, k : k + 1] == expert).astype(F32)
        count_t = jnp.dot(
            jnp.broadcast_to(hit_t, (slots, flat)).astype(BF16), upper, preferred_element_type=F32
        )
        slot = iota((slots, flat), 0)
        want = (slot % CAP + 1).astype(F32)
        ok = (slot // CAP == iota((slots, flat), 1) // per_step) & (count_t == want)
        select.append((ok.astype(F32) * hit_t).astype(BF16))
        count = jnp.dot(
            lower, jnp.broadcast_to(hit, (flat, slots)).astype(BF16), preferred_element_type=F32
        )
        slot = iota((flat, slots), 1)
        want = (slot % CAP + 1).astype(F32)
        ok = (slot // CAP == iota((flat, slots), 0) // per_step) & (count == want)
        spread.append((ok.astype(F32) * hit).astype(BF16))
    id_wide = jnp.concatenate(
        [jnp.broadcast_to(choice[:, k : k + 1], (flat, 128)) for k in range(top)], axis=1
    ).astype(F32).astype(BF16)
    for expert in range(row_size):
        id_stage[expert] = jnp.dot(
            select[expert], id_wide, preferred_element_type=F32
        ).astype(BF16)

    loads[0].wait()
    pl.semaphore_wait(barrier, len(peers))
    id_copies = []
    for a in range(1, row_size):
        copy = pltpu.make_async_remote_copy(
            src_ref=id_stage.at[lax.rem(row + a, row_size)],
            dst_ref=ids.at[row],
            send_sem=si.at[a],
            recv_sem=ri.at[a],
            device_id=at(a, 0),
            device_id_type=MESH,
        )
        copy.start()
        id_copies.append(copy)
    ids[row] = id_stage[row]
    first = {}
    for off in far_first(n):
        to = lax.rem(me + off, n)
        send1[off] = jnp.dot(
            scanned[...], out_weight[:, cols(to)], preferred_element_type=F32
        ).astype(BF16)
        first[off] = pltpu.make_async_remote_copy(
            src_ref=send1.at[off],
            dst_ref=recv1.at[off],
            send_sem=s1.at[off],
            recv_sem=r1.at[off],
            device_id=at(0, off),
            device_id_type=MESH,
        )
        first[off].start()
    total = stream[...].astype(F32) + jnp.dot(
        scanned[...], out_weight[:, cols(me)], preferred_element_type=F32
    )
    for off in reversed(far_first(n)):
        first[off].wait_recv()
        total = total + recv1[off].astype(F32)
    after = total.astype(BF16)

    for expert in range(row_size):
        stage[expert] = jnp.dot(select[expert], after, preferred_element_type=F32).astype(BF16)
    second = []
    for a, b in reversed(peers):
        copy = pltpu.make_async_remote_copy(
            src_ref=stage.at[lax.rem(row + a, row_size)],
            dst_ref=gathered.at[row, me],
            send_sem=s2.at[a, b],
            recv_sem=r2.at[a, b],
            device_id=at(a, b),
            device_id_type=MESH,
        )
        copy.start()
        second.append(copy)
    gathered[row, me] = stage[row]
    for copy in second:
        copy.wait_recv()
    for copy in id_copies:
        copy.wait_recv()
    for r in range(row_size):
        square = jnp.zeros((slots, 1), F32)
        for m in range(n):
            piece = gathered[r, m].astype(F32)
            square = square + jnp.sum(piece * piece, axis=1, keepdims=True)
        scale = lax.rsqrt(square / full + 1e-05)
        for m in range(n):
            piece = gathered[r, m].astype(F32)
            normed[r * slots : (r + 1) * slots, m * width : (m + 1) * width] = (
                piece * scale * gain[:, m * width : (m + 1) * width]
            ).astype(BF16)
    logits = lax.dot_general(
        normed[...], router[...], (((1,), (1,)), ((), ())), preferred_element_type=F32
    )
    slot_ids = jnp.concatenate([ids[r] for r in range(row_size)], axis=0).astype(F32)
    experts = logits.shape[1]
    column = iota(logits.shape, 1).astype(F32)
    mine = row.astype(F32)
    weight_sum = jnp.zeros((row_size * slots, 1), F32)
    weight_own = jnp.zeros((row_size * slots, 1), F32)
    for k in range(top):
        chosen_id = slot_ids[:, k * 128 : k * 128 + experts]
        chosen = jnp.sum(jnp.where(chosen_id == column, logits, 0.0), axis=1, keepdims=True)
        weight = jnp.exp(chosen)
        weight_sum = weight_sum + weight
        weight_own = weight_own + jnp.where(chosen_id[:, :1] == mine, weight, 0.0)
    share = weight_own / weight_sum

    loads[1].wait()
    loads[2].wait()

    def gate_up(i, carry):
        span = pl.ds(pl.multiple_of(i * tile, tile), tile)
        x = normed[...]
        g = jnp.dot(x, gate[:, span], preferred_element_type=F32)
        u = jnp.dot(x, up[:, span], preferred_element_type=F32)
        hidden[:, span] = (jax.nn.silu(g) * u).astype(BF16)
        return carry

    lax.fori_loop(0, gate.shape[1] // tile, gate_up, 0)
    loads[3].wait()
    third = []
    for b in far_first(n) + [0]:
        to = lax.rem(me + b, n)
        part = jnp.dot(hidden[...], down[:, cols(to)], preferred_element_type=F32) * share
        for r in range(row_size):
            send2[b, r] = part[r * slots : (r + 1) * slots].astype(BF16)
        for a in range(row_size):
            if a or b:
                copy = pltpu.make_async_remote_copy(
                    src_ref=send2.at[b, lax.rem(row + a, row_size)],
                    dst_ref=recv2.at[row, b],
                    send_sem=s3.at[a, b],
                    recv_sem=r3.at[a, b],
                    device_id=at(a, b),
                    device_id_type=MESH,
                )
                copy.start()
                third.append(copy)
    recv2[row, 0] = send2[0, row]
    for copy in third:
        copy.wait_recv()
    result = after.astype(F32)
    for expert in range(row_size):
        got = recv2[expert, 0].astype(F32)
        for b in range(1, n):
            got = got + recv2[expert, b].astype(F32)
        high = got.astype(BF16)
        low = (got - high.astype(F32)).astype(BF16)
        result = result + (
            jnp.dot(spread[expert], high, preferred_element_type=F32)
            + jnp.dot(spread[expert], low, preferred_element_type=F32)
        )
    o_ref[...] = result.astype(o_ref.dtype)
    for copy in id_copies + list(first.values()) + second + third:
        copy.wait_send()


def tail(n, row_size, steps, scanned, stream, gain, router, picked, out_w, gate_w, up_w, down_w):
    flat, width = stream.shape
    full = out_w.shape[1]
    slots = steps * CAP
    ff = gate_w.shape[2]
    tile = 256 if ff % 256 == 0 else 128
    dma = pltpu.SemaphoreType.DMA
    vmem = pl.BlockSpec(memory_space=pltpu.VMEM)
    hbm = pl.BlockSpec(memory_space=pl.ANY)
    return pl.pallas_call(
        functools.partial(tail_kernel, n, row_size, steps, tile),
        out_shape=jax.ShapeDtypeStruct((flat, width), BF16),
        in_specs=[vmem] * 6 + [hbm] * 4,
        out_specs=vmem,
        scratch_shapes=[
            pltpu.VMEM(out_w.shape, BF16),
            pltpu.VMEM(gate_w.shape[1:], BF16),
            pltpu.VMEM(up_w.shape[1:], BF16),
            pltpu.VMEM(down_w.shape[1:], BF16),
            pltpu.VMEM((n, flat, width), BF16),
            pltpu.VMEM((n, flat, width), BF16),
            pltpu.VMEM((row_size, slots, width), BF16),
            pltpu.VMEM((row_size, n, slots, width), BF16),
            pltpu.VMEM((row_size, slots, 128 * picked.shape[1]), BF16),
            pltpu.VMEM((row_size, slots, 128 * picked.shape[1]), BF16),
            pltpu.VMEM((row_size * slots, full), BF16),
            pltpu.VMEM((row_size * slots, ff), BF16),
            pltpu.VMEM((n, row_size, slots, width), BF16),
            pltpu.VMEM((row_size, n, slots, width), BF16),
            dma((4,)),
            dma((n,)),
            dma((n,)),
            dma((row_size, n)),
            dma((row_size, n)),
            dma((row_size,)),
            dma((row_size,)),
            dma((row_size, n)),
            dma((row_size, n)),
        ],
        compiler_params=pltpu.CompilerParams(
            collective_id=1, has_side_effects=True, vmem_limit_bytes=56 * 1024 * 1024
        ),
        name="tail",
    )(
        scanned,
        stream,
        gain.reshape(1, -1),
        router,
        picked,
        jnp.transpose(picked),
        out_w,
        gate_w,
        up_w,
        down_w,
    )


def on_device(
    stream,
    projected,
    conv_state,
    scan_state,
    conv_weight,
    conv_bias,
    state_proj,
    step_proj,
    step_bias,
    decay_log,
    skip_gain,
    out_weight,
    norm_gain,
    router,
    expert_gate,
    expert_up,
    expert_down,
    expert_ids,
):
    step_count, row_count, width_local = stream.shape
    inner_local = projected.shape[3]
    kernel_size = conv_weight.shape[0]
    rank_size = step_proj.shape[0]
    state_size = decay_log.shape[0]
    flat_rows = step_count * row_count
    inputs = projected[:, :, 0, :]
    gate_side = projected[:, :, 1, :]
    history = jnp.concatenate(
        [conv_state.astype(jnp.float32), jnp.transpose(inputs, (1, 0, 2)).astype(jnp.float32)],
        axis=1,
    )
    conv_list = []
    for step_no in range(step_count):
        window = history[:, step_no : step_no + kernel_size, :]
        conv_list.append(
            jax.nn.silu(jnp.sum(window * conv_weight[None], axis=1) + conv_bias).astype(
                jnp.bfloat16
            )
        )
    convolved = jnp.stack(conv_list)
    local_proj = jnp.dot(
        convolved.reshape(flat_rows, inner_local), state_proj, preferred_element_type=jnp.float32
    )
    projections = sum_over_mp(lax.axis_size("mp"), local_proj).reshape(
        step_count, row_count, -1
    )
    low_rank = projections[..., :rank_size].astype(jnp.bfloat16)
    input_gain = projections[..., rank_size : rank_size + state_size].astype(jnp.float32)
    output_gain = projections[..., rank_size + state_size :].astype(jnp.float32)
    timestep = jax.nn.softplus(
        jnp.dot(
            low_rank.reshape(flat_rows, rank_size), step_proj, preferred_element_type=jnp.float32
        ).reshape(step_count, row_count, inner_local)
        + step_bias
    )
    decay_rates = jnp.exp(decay_log)
    carried = scan_state
    outputs = []
    for step_no in range(step_count):
        current = convolved[step_no].astype(jnp.float32)
        delta_now = timestep[step_no]
        decay_now = jnp.exp(-delta_now[:, None, :] * decay_rates[None])
        carried = (
            decay_now * carried
            + (delta_now * current)[:, None, :] * input_gain[step_no][:, :, None]
        )
        readout = jnp.sum(output_gain[step_no][:, :, None] * carried, axis=1) + skip_gain * current
        outputs.append(
            (readout * jax.nn.silu(gate_side[step_no].astype(jnp.float32))).astype(jnp.bfloat16)
        )
    scanned = jnp.stack(outputs).reshape(flat_rows, inner_local)
    mixed_out = tail(
        lax.axis_size("mp"),
        lax.axis_size("row"),
        step_count,
        scanned,
        stream.reshape(flat_rows, width_local),
        norm_gain,
        router,
        expert_ids.reshape(flat_rows, -1),
        out_weight,
        expert_gate,
        expert_up,
        expert_down,
    ).reshape(step_count, row_count, width_local)
    return (mixed_out, carried)


def solution(mesh):
    return jax.shard_map(
        on_device,
        mesh=mesh,
        in_specs=(
            P(None, ("groups", "row"), "mp"),
            P(None, ("groups", "row"), None, "mp"),
            P(("groups", "row"), None, "mp"),
            P(("groups", "row"), None, "mp"),
            P(None, "mp"),
            P("mp"),
            P("mp", None),
            P(None, "mp"),
            P("mp"),
            P(None, "mp"),
            P("mp"),
            P("mp", None),
            P(),
            P(),
            P("row", None, "mp"),
            P("row", None, "mp"),
            P("row", "mp", None),
            P(None, ("groups", "row"), None),
        ),
        out_specs=(P(None, ("groups", "row"), "mp"), P(("groups", "row"), None, "mp")),
        check_vma=False,
    )
```

time: 297 us -> 93.7 us (0.32)
  waiting for transfers between devices: 141 us -> 0 us
  blocking collectives: 101 us -> 0 us
  Pallas kernels: 0 us -> 76.8 us
  matrix products: 21.6 us -> 1.85 us
  between operations: 14.4 us -> 0.85 us
  other arithmetic: 13.2 us -> 8.94 us
    psum x1 -> x0, blocking collectives: 92.4 us -> none  [on_device(): after_full = lax.psum(placed, 'mp').astype(jnp.bfloat16)]
    pallas_call x0 -> x2, Pallas kernels: none -> 76.8 us  [the longest x1 59.4 us: tail(): pl.pallas_call(functools.partial(tail_kernel, n, row_size, steps, tile),...]
    psum x1 -> x0, waiting for transfers between devices: 72.3 us -> none  [on_device(): projections = lax.psum(local_proj, 'mp').reshape(step_count, row_count, -1)]
    reduce_scatter x1 -> x0, waiting for transfers between devices: 69.1 us -> none  [on_device(): combined = lax.psum_scatter(combined, 'mp', scatter_dimension=1, tiled=True)]
    dot_general x8 -> x0, matrix products: 19 us -> none  [the longest x1 6.97 us: expert_apply(): jnp.dot(tokens_in, gate_weight, preferred_element_type=jnp.float32)]
    all_to_all x2 -> x0, blocking collectives: 8.32 us -> none  [the longest x1 4.16 us: on_device(): lax.all_to_all(outgoing, 'row', split_axis=0, concat_axis=0, tiled=True)]
  transfers between devices with their start and end apart: 2 -> 0, of which waited for: 2 -> 0; matrix products, arithmetic and copies ran while one was open for 0% -> 0% of each run, Pallas kernels for 0% -> 0%
where the time goes in v1:
time: 93.7 us; the launch traced here: 93.5 us
  Pallas kernels  76.8 us (82%)
  other arithmetic  8.94 us (10%)
  local copies, waits for them, and re-layouts  5.01 us (5%)
  matrix products  1.85 us (2%)
    pallas_call x1, Pallas kernels, tail(): pl.pallas_call(functools.partial(tail_kernel, n, row_size, steps, tile),...  59.4 us
    pallas_call x1, Pallas kernels, sum_over_mp(): pl.pallas_call(functools.partial(sum_kernel, n), out_shape=jax.ShapeDtype...  17.4 us
    reduce_sum x1, other arithmetic, on_device(): jnp.sum(output_gain[step_no][:, :, None] * carried, axis=1)  4.59 us
    unnamed x23, local copies, waits for them, and re-layouts  2.84 us

profile of v1, /device:TPU:0, one launch (start us, length us, event | category | flops | bytes accessed | tf_op | source)
XLA Modules:
  0.0 93.5 jit_solution(13562758851697069212)
XLA Ops:
  0.6 0.0 copy-start
  0.6 0.0 copy-start.4
  0.7 0.0 copy-start.8
  0.7 0.0 copy-start.9
  0.7 1.2 %copy.36 = bf16[2,64,1,1024]{3,1,0,2:T(8,128)(2,1)S(1)} copy(bf16[2,64,1,1024]{3,2,1,0:T(2,128)(2,1)} %bitcast.73) | data formatting | bytes 524288
  1.9 1.1 %maximum_convert_fusion = f32[64,5,1024]{2,0,1:T(8,128)S(1)} fusion(bf16[64,2,1024]{2,0,1:T(8,128)(2,1)S(1)} %bitcast.75, bf16[64,3,1024]{2,0,1:T(8,128)(2,1)} %param.20), kind=kLoop, calls=%fused_computation.11 | loop fusion | flops 655360 | bytes 1966080 | tf_op jit(solution)/shard_map/concatenate | solution.py:416
  3.0 0.0 copy-start.3
  3.0 0.9 %fusion.1 = (f32[64,1024]{1,0:T(8,128)S(1)}, f32[64,1024]{1,0:T(8,128)S(1)}) fusion(f32[64,5,1024]{2,0,1:T(8,128)S(1)} %maximum_convert_fusion, f32[4,1024]{1,0:T(4,128)} %param.22), kind=kLoop, calls=%fused_computation.10 | loop fusion | flops 917504 | bytes 2637824 | tf_op jit(solution)/shard_map/reduce_sum | solution.py:424
  3.9 0.0 copy-done.4
  3.9 0.2 multiply_convert_fusion.3
  4.1 0.0 copy-done
  4.2 0.3 convolution_convert_fusion
  4.5 0.8 copy.21
  5.2 17.4 %sum_over_mp.1 = bf16[8,16,288]{2,1,0:T(8,128)(2,1)} custom-call(bf16[8,16,288]{2,1,0:T(8,128)(2,1)} %bitcast.78), custom_call_target="tpu_custom_call" | custom-call | tf_op jit(solution)/shard_map/sum_over_mp/pallas_call | solution.py:68
  22.6 0.0 copy-start.1
  22.6 1.0 %slice_convert_fusion = (f32[2,64,16]{2,1,0:T(8,128)S(1)}, f32[2,64,16]{2,1,0:T(8,128)S(1)}) fusion(bf16[2,64,288]{2,1,0:T(8,128)(2,1)} %bitcast.79), kind=kLoop, calls=%fused_computation.50 | loop fusion | flops 4096 | bytes 24576 | tf_op jit(solution)/shard_map/convert_element_type | solution.py:436
  23.7 0.0 copy-done.8
  23.7 0.0 copy-done.9
  23.7 1.5 %compare_select_fusion = f32[2,64,1024]{2,1,0:T(8,128)S(1)} fusion(bf16[256,1024]{1,0:T(8,128)(2,1)S(1)} %copy-done.8, f32[1024]{0:T(1024)S(1)} %copy-done.9, bf16[2,64,288]{2,1,0:T(8,128)(2,1)} %bitcast.80), kind=kOutput, calls=%fused_computation.4 | convolution fusion | flops 68026368 | bytes 1118208 | tf_op jit(solution)/shard_map/dot_general | solution.py:439
  25.2 0.2 convert_multiply_fusion.3
  25.4 0.0 copy-done.3
  25.4 0.0 copy-done.1
  25.4 0.0 copy-start.2
  25.4 0.0 copy-start.6
  25.5 0.0 copy-start.7
  25.5 4.6 %multiply_reduce_fusion = (f32[64,1024]{1,0:T(8,128)S(1)}, f32[64,16,1024]{2,1,0:T(8,128)}, f32[64,1024]{1,0:T(8,128)S(1)}) fusion(f32[64,16]{1,0:T(8,128)S(1)} %get-tuple-element.23, f32[64,16]{1,0:T(8,128)S(1)} %get-tuple-element.18, f32[64,1024]{1,0:T(8,128)S(1)} %get-tuple-element.8, f32[64,16]{1,0:T(8,128)S(1)} %get-tuple-element.17, ...), kind=kLoop, calls=%fused_computation | loop fusion | flops 12451840 | bytes 10043392 | tf_op jit(solution)/shard_map/reduce_sum | solution.py:455
  30.1 0.0 copy-done.2
  30.1 0.6 fusion.18
  30.6 0.0 copy-done.6
  30.6 0.2 fusion.14
  30.9 0.7 pad_maximum_fusion.1
  31.6 0.0 copy-done.7
  31.6 0.1 reshape.383
  31.7 0.0 copy-start.5
  31.7 0.7 copy.25.picked
  32.4 0.0 copy-done.5
  32.4 59.4 %tail.1 = bf16[128,512]{1,0:T(8,128)(2,1)} custom-call(bf16[128,1024]{1,0:T(8,128)(2,1)} %bitcast.74, bf16[128,512]{1,0:T(8,128)(2,1)} %bitcast.81, f32[1,4096]{1,0:T(1,128)} %bitcast.82, bf16[16,4096]{1,0:T(8,128)(2,1)} %router.1, s32[128,2]{1,0:T(8,128)} %copy.25.picked, s32[2,128]{1,0:T(2,128)} %bitcast.83, bf16[1024,4096]{1,0:T(8,128)(2,1)} %out_hbm.1, ...), custom_call_target="tpu_custom_call" | custom-call | tf_op jit(solution)/shard_map/tail/pallas_call | solution.py:340
  91.9 1.6 %copy.38 = bf16[2,64,512]{2,1,0:T(8,128)(2,1)} copy(bf16[2,64,512]{2,1,0:T(8,128)(2,1)} %bitcast.77) | data formatting | bytes 262144
  (4 shorter events, 0.1 us)
Async XLA Ops:
  0.6 3.5 %copy-start = (bf16[1024,288]{0,1:T(8,128)(2,1)S(1)}, bf16[1024,288]{0,1:T(8,128)(2,1)}, u32[]{:S(2)}) copy-start(bf16[1024,288]{0,1:T(8,128)(2,1)} %param.24) | copy-start | bytes 1769476
  0.6 3.3 %copy-start.4 = (f32[1024]{0:T(1024)S(1)}, f32[1024]{0:T(1024)}, u32[]{:S(2)}) copy-start(f32[1024]{0:T(1024)} %param.23) | copy-start | bytes 12292
  0.7 23.0 %copy-start.8 = (bf16[256,1024]{1,0:T(8,128)(2,1)S(1)}, bf16[256,1024]{1,0:T(8,128)(2,1)}, u32[]{:S(2)}) copy-start(bf16[256,1024]{1,0:T(8,128)(2,1)} %param.25) | copy-start | bytes 1572868
  0.7 23.0 %copy-start.9 = (f32[1024]{0:T(1024)S(1)}, f32[1024]{0:T(1024)}, u32[]{:S(2)}) copy-start(f32[1024]{0:T(1024)} %param.26) | copy-start | bytes 12292
  3.0 22.4 %copy-start.3 = (f32[16,1024]{1,0:T(8,128)S(1)}, f32[16,1024]{1,0:T(8,128)}, u32[]{:S(2)}) copy-start(f32[16,1024]{1,0:T(8,128)} %param.27) | copy-start | bytes 196612
  22.6 2.8 %copy-start.1 = (f32[64,16,1024]{2,1,0:T(8,128)S(1)}, f32[64,16,1024]{2,1,0:T(8,128)}, u32[]{:S(2)}) copy-start(f32[64,16,1024]{2,1,0:T(8,128)} %param.21) | copy-start | bytes 12582916
  25.4 4.6 %copy-start.2 = (bf16[2,64,2,1024]{3,2,1,0:T(2,128)(2,1)S(1)}, bf16[2,64,2,1024]{3,2,1,0:T(2,128)(2,1)}, u32[]{:S(2)}) copy-start(bf16[2,64,2,1024]{3,2,1,0:T(2,128)(2,1)} %param.19) | copy-start | bytes 1572868
  25.4 5.2 %copy-start.6 = (f32[1024]{0:T(1024)S(1)}, f32[1024]{0:T(1024)}, u32[]{:S(2)}) copy-start(f32[1024]{0:T(1024)} %param.28) | copy-start | bytes 12292
  25.5 6.2 %copy-start.7 = (s32[2,64,2]{1,2,0:T(2,128)S(1)}, s32[2,64,2]{1,2,0:T(2,128)}, u32[]{:S(2)}) copy-start(s32[2,64,2]{1,2,0:T(2,128)} %param.35) | copy-start | bytes 3076
  31.7 0.7 copy-start.5

commit v2 on v1

--- a/solution.py
+++ b/solution.py
@@ -123,6 +123,16 @@
     ri,
     s3,
     r3,
+    cross1,
+    met1,
+    cross2,
+    met2,
+    sc1,
+    rc1,
+    sf,
+    rf,
+    sc2,
+    rc2,
 ):
     me = lax.axis_index("mp")
     row = lax.axis_index("row")
@@ -130,10 +140,16 @@
     full = normed.shape[1]
     slots = steps * CAP
     per_step = flat // steps
-    peers = [(a, b) for b in [0] + far_first(n) for a in range(row_size) if a or b]
+    pairs = n // 2
+    side = lax.rem(me, 2)
+    place = me // 2
+    order = far_first(pairs) + [0]
+    peers = [(a, b) for b in reversed(order) for a in range(row_size) if a or b]
 
     def at(a, b):
-        return {"row": lax.rem(row + a, row_size), "mp": lax.rem(me + b, n)}
+        return {"row": lax.rem(row + a, row_size), "mp": lax.rem(place + b, pairs) * 2 + side}
+
+    partner = {"row": row, "mp": place * 2 + 1 - side}
 
     def cols(index):
         return pl.ds(pl.multiple_of(index * width, width), width)
@@ -154,6 +170,7 @@
     barrier = pltpu.get_barrier_semaphore()
     for a, b in peers:
         pl.semaphore_signal(barrier, inc=1, device_id=at(a, b), device_id_type=MESH)
+    pl.semaphore_signal(barrier, inc=1, device_id=partner, device_id_type=MESH)
 
     def iota(shape, dim):
         return lax.broadcasted_iota(jnp.int32, shape, dim)
@@ -194,7 +211,7 @@
         ).astype(BF16)
 
     loads[0].wait()
-    pl.semaphore_wait(barrier, len(peers))
+    pl.semaphore_wait(barrier, len(peers) + 1)
     id_copies = []
     for a in range(1, row_size):
         copy = pltpu.make_async_remote_copy(
@@ -208,34 +225,50 @@
         copy.start()
         id_copies.append(copy)
     ids[row] = id_stage[row]
-    first = {}
-    for off in far_first(n):
-        to = lax.rem(me + off, n)
-        send1[off] = jnp.dot(
+    across = {}
+    for off in order:
+        to = lax.rem(place + off, pairs) * 2 + 1 - side
+        cross1[off] = jnp.dot(
             scanned[...], out_weight[:, cols(to)], preferred_element_type=F32
         ).astype(BF16)
-        first[off] = pltpu.make_async_remote_copy(
-            src_ref=send1.at[off],
-            dst_ref=recv1.at[off],
-            send_sem=s1.at[off],
-            recv_sem=r1.at[off],
-            device_id=at(0, off),
-            device_id_type=MESH,
-        )
-        first[off].start()
-    total = stream[...].astype(F32) + jnp.dot(
-        scanned[...], out_weight[:, cols(me)], preferred_element_type=F32
-    )
-    for off in reversed(far_first(n)):
+        across[off] = pltpu.make_async_remote_copy(
+            src_ref=cross1.at[off],
+            dst_ref=met1.at[off],
+            send_sem=sc1.at[off],
+            recv_sem=rc1.at[off],
+            device_id=partner,
+            device_id_type=MESH,
+        )
+        across[off].start()
+    first = {}
+    for off in order:
+        to = lax.rem(place + off, pairs) * 2 + side
+        part = jnp.dot(scanned[...], out_weight[:, cols(to)], preferred_element_type=F32)
+        across[off].wait_recv()
+        part = part + met1[off].astype(F32)
+        if off:
+            send1[off] = part.astype(BF16)
+            first[off] = pltpu.make_async_remote_copy(
+                src_ref=send1.at[off],
+                dst_ref=recv1.at[off],
+                send_sem=s1.at[off],
+                recv_sem=r1.at[off],
+                device_id=at(0, off),
+                device_id_type=MESH,
+            )
+            first[off].start()
+        else:
+            total = stream[...].astype(F32) + part
+    for off in order[:-1]:
         first[off].wait_recv()
         total = total + recv1[off].astype(F32)
     after = total.astype(BF16)
 
     for expert in range(row_size):
         stage[expert] = jnp.dot(select[expert], after, preferred_element_type=F32).astype(BF16)
-    second = []
+    second = {}
     for a, b in reversed(peers):
-        copy = pltpu.make_async_remote_copy(
+        second[a, b] = pltpu.make_async_remote_copy(
             src_ref=stage.at[lax.rem(row + a, row_size)],
             dst_ref=gathered.at[row, me],
             send_sem=s2.at[a, b],
@@ -243,10 +276,28 @@
             device_id=at(a, b),
             device_id_type=MESH,
         )
+        second[a, b].start()
+    gathered[row, me] = stage[row]
+    onward = []
+    for a, b in [(0, 0)] + peers:
+        r = lax.rem(row - a + row_size, row_size)
+        m = lax.rem(place - b + pairs, pairs) * 2 + side
+        if a or b:
+            second[a, b].wait_recv()
+            block = gathered.at[r, m]
+        else:
+            block = stage.at[row]
+        copy = pltpu.make_async_remote_copy(
+            src_ref=block,
+            dst_ref=gathered.at[r, m],
+            send_sem=sf.at[a, b],
+            recv_sem=rf.at[a, b],
+            device_id=partner,
+            device_id_type=MESH,
+        )
         copy.start()
-        second.append(copy)
-    gathered[row, me] = stage[row]
-    for copy in second:
+        onward.append(copy)
+    for copy in onward:
         copy.wait_recv()
     for copy in id_copies:
         copy.wait_recv()
@@ -291,10 +342,27 @@
 
     lax.fori_loop(0, gate.shape[1] // tile, gate_up, 0)
     loads[3].wait()
+    back = {}
+    for b in order:
+        to = lax.rem(place + b, pairs) * 2 + 1 - side
+        cross2[b] = (
+            jnp.dot(hidden[...], down[:, cols(to)], preferred_element_type=F32) * share
+        ).astype(BF16)
+        back[b] = pltpu.make_async_remote_copy(
+            src_ref=cross2.at[b],
+            dst_ref=met2.at[b],
+            send_sem=sc2.at[b],
+            recv_sem=rc2.at[b],
+            device_id=partner,
+            device_id_type=MESH,
+        )
+        back[b].start()
     third = []
-    for b in far_first(n) + [0]:
-        to = lax.rem(me + b, n)
+    for b in order:
+        to = lax.rem(place + b, pairs) * 2 + side
         part = jnp.dot(hidden[...], down[:, cols(to)], preferred_element_type=F32) * share
+        back[b].wait_recv()
+        part = part + met2[b].astype(F32)
         for r in range(row_size):
             send2[b, r] = part[r * slots : (r + 1) * slots].astype(BF16)
         for a in range(row_size):
@@ -315,7 +383,7 @@
     result = after.astype(F32)
     for expert in range(row_size):
         got = recv2[expert, 0].astype(F32)
-        for b in range(1, n):
+        for b in range(1, pairs):
             got = got + recv2[expert, b].astype(F32)
         high = got.astype(BF16)
         low = (got - high.astype(F32)).astype(BF16)
@@ -324,7 +392,8 @@
             + jnp.dot(spread[expert], low, preferred_element_type=F32)
         )
     o_ref[...] = result.astype(o_ref.dtype)
-    for copy in id_copies + list(first.values()) + second + third:
+    sent = [across, first, second, back]
+    for copy in id_copies + [c for group in sent for c in group.values()] + onward + third:
         copy.wait_send()
 
 
@@ -334,6 +403,7 @@
     slots = steps * CAP
     ff = gate_w.shape[2]
     tile = 256 if ff % 256 == 0 else 128
+    pairs = n // 2
     dma = pltpu.SemaphoreType.DMA
     vmem = pl.BlockSpec(memory_space=pltpu.VMEM)
     hbm = pl.BlockSpec(memory_space=pl.ANY)
@@ -347,25 +417,35 @@
             pltpu.VMEM(gate_w.shape[1:], BF16),
             pltpu.VMEM(up_w.shape[1:], BF16),
             pltpu.VMEM(down_w.shape[1:], BF16),
-            pltpu.VMEM((n, flat, width), BF16),
-            pltpu.VMEM((n, flat, width), BF16),
+            pltpu.VMEM((pairs, flat, width), BF16),
+            pltpu.VMEM((pairs, flat, width), BF16),
             pltpu.VMEM((row_size, slots, width), BF16),
             pltpu.VMEM((row_size, n, slots, width), BF16),
             pltpu.VMEM((row_size, slots, 128 * picked.shape[1]), BF16),
             pltpu.VMEM((row_size, slots, 128 * picked.shape[1]), BF16),
             pltpu.VMEM((row_size * slots, full), BF16),
             pltpu.VMEM((row_size * slots, ff), BF16),
-            pltpu.VMEM((n, row_size, slots, width), BF16),
-            pltpu.VMEM((row_size, n, slots, width), BF16),
+            pltpu.VMEM((pairs, row_size, slots, width), BF16),
+            pltpu.VMEM((row_size, pairs, slots, width), BF16),
             dma((4,)),
-            dma((n,)),
-            dma((n,)),
-            dma((row_size, n)),
-            dma((row_size, n)),
+            dma((pairs,)),
+            dma((pairs,)),
+            dma((row_size, pairs)),
+            dma((row_size, pairs)),
             dma((row_size,)),
             dma((row_size,)),
-            dma((row_size, n)),
-            dma((row_size, n)),
+            dma((row_size, pairs)),
+            dma((row_size, pairs)),
+            pltpu.VMEM((pairs, flat, width), BF16),
+            pltpu.VMEM((pairs, flat, width), BF16),
+            pltpu.VMEM((pairs, row_size * slots, width), BF16),
+            pltpu.VMEM((pairs, row_size * slots, width), BF16),
+            dma((pairs,)),
+            dma((pairs,)),
+            dma((row_size, pairs)),
+            dma((row_size, pairs)),
+            dma((pairs,)),
+            dma((pairs,)),
         ],
         compiler_params=pltpu.CompilerParams(
             collective_id=1, has_side_effects=True, vmem_limit_bytes=56 * 1024 * 1024

time: 93.7 us -> 83.6 us (0.89)
  Pallas kernels: 76.8 us -> 66.7 us
    pallas_call x1, Pallas kernels: 59.4 us -> 49.3 us  [tail(): pl.pallas_call(functools.partial(tail_kernel, n, row_size, steps, tile),...]
where the time goes in v2:
time: 83.6 us; the launch traced here: 83.4 us
  Pallas kernels  66.7 us (80%)
  other arithmetic  8.94 us (11%)
  local copies, waits for them, and re-layouts  5.01 us (6%)
  matrix products  1.85 us (2%)
  between operations  0.85 us (1%)
    pallas_call x1, Pallas kernels, tail(): pl.pallas_call(functools.partial(tail_kernel, n, row_size, steps, tile),...  49.3 us
    pallas_call x1, Pallas kernels, sum_over_mp(): pl.pallas_call(functools.partial(sum_kernel, n), out_shape=jax.ShapeDtype...  17.4 us
    reduce_sum x1, other arithmetic, on_device(): jnp.sum(output_gain[step_no][:, :, None] * carried, axis=1)  4.59 us
    unnamed x23, local copies, waits for them, and re-layouts  2.84 us

profile of v2, /device:TPU:0, one launch (start us, length us, event | category | flops | bytes accessed | tf_op | source)
XLA Modules:
  0.0 83.4 jit_solution(17287090859054456161)
XLA Ops:
  0.6 0.0 copy-start
  0.6 0.0 copy-start.4
  0.7 0.0 copy-start.8
  0.7 0.0 copy-start.9
  0.7 1.2 %copy.36 = bf16[2,64,1,1024]{3,1,0,2:T(8,128)(2,1)S(1)} copy(bf16[2,64,1,1024]{3,2,1,0:T(2,128)(2,1)} %bitcast.73) | data formatting | bytes 524288
  1.9 1.1 %maximum_convert_fusion = f32[64,5,1024]{2,0,1:T(8,128)S(1)} fusion(bf16[64,2,1024]{2,0,1:T(8,128)(2,1)S(1)} %bitcast.75, bf16[64,3,1024]{2,0,1:T(8,128)(2,1)} %param.20), kind=kLoop, calls=%fused_computation.11 | loop fusion | flops 655360 | bytes 1966080 | tf_op jit(solution)/shard_map/concatenate | solution.py:496
  3.0 0.0 copy-start.3
  3.0 0.9 %fusion.1 = (f32[64,1024]{1,0:T(8,128)S(1)}, f32[64,1024]{1,0:T(8,128)S(1)}) fusion(f32[64,5,1024]{2,0,1:T(8,128)S(1)} %maximum_convert_fusion, f32[4,1024]{1,0:T(4,128)} %param.22), kind=kLoop, calls=%fused_computation.10 | loop fusion | flops 917504 | bytes 2637824 | tf_op jit(solution)/shard_map/reduce_sum | solution.py:504
  3.9 0.0 copy-done.4
  3.9 0.2 multiply_convert_fusion.3
  4.1 0.0 copy-done
  4.2 0.3 convolution_convert_fusion
  4.5 0.8 copy.21
  5.2 17.4 %sum_over_mp.1 = bf16[8,16,288]{2,1,0:T(8,128)(2,1)} custom-call(bf16[8,16,288]{2,1,0:T(8,128)(2,1)} %bitcast.78), custom_call_target="tpu_custom_call" | custom-call | tf_op jit(solution)/shard_map/sum_over_mp/pallas_call | solution.py:68
  22.6 0.0 copy-start.1
  22.6 1.0 %slice_convert_fusion = (f32[2,64,16]{2,1,0:T(8,128)S(1)}, f32[2,64,16]{2,1,0:T(8,128)S(1)}) fusion(bf16[2,64,288]{2,1,0:T(8,128)(2,1)} %bitcast.79), kind=kLoop, calls=%fused_computation.50 | loop fusion | flops 4096 | bytes 24576 | tf_op jit(solution)/shard_map/convert_element_type | solution.py:516
  23.7 0.0 copy-done.8
  23.7 0.0 copy-done.9
  23.7 1.5 %compare_select_fusion = f32[2,64,1024]{2,1,0:T(8,128)S(1)} fusion(bf16[256,1024]{1,0:T(8,128)(2,1)S(1)} %copy-done.8, f32[1024]{0:T(1024)S(1)} %copy-done.9, bf16[2,64,288]{2,1,0:T(8,128)(2,1)} %bitcast.80), kind=kOutput, calls=%fused_computation.4 | convolution fusion | flops 68026368 | bytes 1118208 | tf_op jit(solution)/shard_map/dot_general | solution.py:519
  25.2 0.2 convert_multiply_fusion.3
  25.4 0.0 copy-done.3
  25.4 0.0 copy-done.1
  25.4 0.0 copy-start.2
  25.4 0.0 copy-start.6
  25.5 0.0 copy-start.7
  25.5 4.6 %multiply_reduce_fusion = (f32[64,1024]{1,0:T(8,128)S(1)}, f32[64,16,1024]{2,1,0:T(8,128)}, f32[64,1024]{1,0:T(8,128)S(1)}) fusion(f32[64,16]{1,0:T(8,128)S(1)} %get-tuple-element.23, f32[64,16]{1,0:T(8,128)S(1)} %get-tuple-element.18, f32[64,1024]{1,0:T(8,128)S(1)} %get-tuple-element.8, f32[64,16]{1,0:T(8,128)S(1)} %get-tuple-element.17, ...), kind=kLoop, calls=%fused_computation | loop fusion | flops 12451840 | bytes 10043392 | tf_op jit(solution)/shard_map/reduce_sum | solution.py:535
  30.1 0.0 copy-done.2
  30.1 0.6 fusion.18
  30.6 0.0 copy-done.6
  30.6 0.2 fusion.14
  30.9 0.7 pad_maximum_fusion.1
  31.6 0.0 copy-done.7
  31.6 0.1 reshape.383
  31.7 0.0 copy-start.5
  31.7 0.7 copy.25.picked
  32.4 0.0 copy-done.5
  32.4 49.3 %tail.1 = bf16[128,512]{1,0:T(8,128)(2,1)} custom-call(bf16[128,1024]{1,0:T(8,128)(2,1)} %bitcast.74, bf16[128,512]{1,0:T(8,128)(2,1)} %bitcast.81, f32[1,4096]{1,0:T(1,128)} %bitcast.82, bf16[16,4096]{1,0:T(8,128)(2,1)} %router.1, s32[128,2]{1,0:T(8,128)} %copy.25.picked, s32[2,128]{1,0:T(2,128)} %bitcast.83, bf16[1024,4096]{1,0:T(8,128)(2,1)} %out_hbm.1, ...), custom_call_target="tpu_custom_call" | custom-call | tf_op jit(solution)/shard_map/tail/pallas_call | solution.py:410
  81.8 1.6 %copy.38 = bf16[2,64,512]{2,1,0:T(8,128)(2,1)} copy(bf16[2,64,512]{2,1,0:T(8,128)(2,1)} %bitcast.77) | data formatting | bytes 262144
  (4 shorter events, 0.1 us)
Async XLA Ops:
  0.6 3.5 %copy-start = (bf16[1024,288]{0,1:T(8,128)(2,1)S(1)}, bf16[1024,288]{0,1:T(8,128)(2,1)}, u32[]{:S(2)}) copy-start(bf16[1024,288]{0,1:T(8,128)(2,1)} %param.24) | copy-start | bytes 1769476
  0.6 3.3 %copy-start.4 = (f32[1024]{0:T(1024)S(1)}, f32[1024]{0:T(1024)}, u32[]{:S(2)}) copy-start(f32[1024]{0:T(1024)} %param.23) | copy-start | bytes 12292
  0.7 23.0 %copy-start.8 = (bf16[256,1024]{1,0:T(8,128)(2,1)S(1)}, bf16[256,1024]{1,0:T(8,128)(2,1)}, u32[]{:S(2)}) copy-start(bf16[256,1024]{1,0:T(8,128)(2,1)} %param.25) | copy-start | bytes 1572868
  0.7 23.0 %copy-start.9 = (f32[1024]{0:T(1024)S(1)}, f32[1024]{0:T(1024)}, u32[]{:S(2)}) copy-start(f32[1024]{0:T(1024)} %param.26) | copy-start | bytes 12292
  3.0 22.4 %copy-start.3 = (f32[16,1024]{1,0:T(8,128)S(1)}, f32[16,1024]{1,0:T(8,128)}, u32[]{:S(2)}) copy-start(f32[16,1024]{1,0:T(8,128)} %param.27) | copy-start | bytes 196612
  22.6 2.8 %copy-start.1 = (f32[64,16,1024]{2,1,0:T(8,128)S(1)}, f32[64,16,1024]{2,1,0:T(8,128)}, u32[]{:S(2)}) copy-start(f32[64,16,1024]{2,1,0:T(8,128)} %param.21) | copy-start | bytes 12582916
  25.4 4.6 %copy-start.2 = (bf16[2,64,2,1024]{3,2,1,0:T(2,128)(2,1)S(1)}, bf16[2,64,2,1024]{3,2,1,0:T(2,128)(2,1)}, u32[]{:S(2)}) copy-start(bf16[2,64,2,1024]{3,2,1,0:T(2,128)(2,1)} %param.19) | copy-start | bytes 1572868
  25.4 5.2 %copy-start.6 = (f32[1024]{0:T(1024)S(1)}, f32[1024]{0:T(1024)}, u32[]{:S(2)}) copy-start(f32[1024]{0:T(1024)} %param.28) | copy-start | bytes 12292
  25.5 6.2 %copy-start.7 = (s32[2,64,2]{1,2,0:T(2,128)S(1)}, s32[2,64,2]{1,2,0:T(2,128)}, u32[]{:S(2)}) copy-start(s32[2,64,2]{1,2,0:T(2,128)} %param.35) | copy-start | bytes 3076
  31.7 0.7 copy-start.5

commit v3 on v2

v3 whole, which is shorter than its diff:
```python
import functools

import jax
import jax.numpy as jnp
from jax import lax
from jax.experimental import pallas as pl
from jax.experimental.pallas import tpu as pltpu
from jax.sharding import PartitionSpec as P

CAP = 16
LANES = 128
MESH = pl.DeviceIdType.MESH
F32 = jnp.float32
BF16 = jnp.bfloat16


def far_first(n):
    return sorted(range(1, n), key=lambda off: -min(off, n - off))


def kernel(
    n,
    row_size,
    tile,
    xz,
    conv_state,
    conv_weight,
    conv_bias,
    state_proj,
    step_proj,
    step_bias,
    decay_log,
    skip_gain,
    stream,
    gain,
    router,
    picked,
    state_hbm,
    out_hbm,
    gate_hbm,
    up_hbm,
    down_hbm,
    o_ref,
    new_state,
    state,
    convolved,
    delta,
    moved,
    readout,
    gain_in,
    gain_out,
    rates,
    part_proj,
    recv_proj,
    own_proj,
    full_proj,
    out_weight,
    gate,
    up,
    down,
    send1,
    recv1,
    stage,
    gathered,
    id_stage,
    ids,
    normed,
    hidden,
    send2,
    recv2,
    cross1,
    met1,
    cross2,
    met2,
    load_sem,
    sa,
    ra,
    sb,
    rb,
    s1,
    r1,
    s2,
    r2,
    si,
    ri,
    s3,
    r3,
    sc1,
    rc1,
    sf,
    rf,
    sc2,
    rc2,
):
    me = lax.axis_index("mp")
    row = lax.axis_index("row")
    steps, rows, width = stream.shape
    flat = steps * rows
    inner = xz.shape[3]
    taps = conv_weight.shape[0]
    rank = step_proj.shape[0]
    entries = decay_log.shape[0]
    full = normed.shape[1]
    slots = steps * CAP
    pairs = n // 2
    side = lax.rem(me, 2)
    place = me // 2
    order = far_first(pairs) + [0]
    peers = [(a, b) for b in reversed(order) for a in range(row_size) if a or b]

    def at(a, b):
        return {"row": lax.rem(row + a, row_size), "mp": lax.rem(place + b, pairs) * 2 + side}

    partner = {"row": row, "mp": place * 2 + 1 - side}

    def along(off):
        return {"row": row, "mp": lax.rem(me + off, n)}

    def cols(index):
        return pl.ds(pl.multiple_of(index * width, width), width)

    loads = [
        pltpu.make_async_copy(src, dst, load_sem.at[k])
        for k, (src, dst) in enumerate(
            [
                (out_hbm, out_weight),
                (gate_hbm.at[0], gate),
                (up_hbm.at[0], up),
                (down_hbm.at[0], down),
                (state_hbm, state),
            ]
        )
    ]
    barrier = pltpu.get_barrier_semaphore()
    for off in far_first(n):
        pl.semaphore_signal(barrier, inc=1, device_id=along(off), device_id_type=MESH)
    others = [(a, b) for a, b in peers if a]
    for a, b in others:
        pl.semaphore_signal(barrier, inc=1, device_id=at(a, b), device_id_type=MESH)
    for k in (4, 0, 1, 2, 3):
        loads[k].start()

    window = [conv_state[k].astype(F32) for k in range(taps - 1)]
    window = window + [xz[0, s].astype(F32) for s in range(steps)]
    local = []
    for s in range(steps):
        total = conv_bias[...]
        for k in range(taps):
            total = total + window[s + k] * conv_weight[k : k + 1, :]
        convolved[s] = jax.nn.silu(total).astype(BF16)
        local.append(
            lax.dot_general(
                convolved[s],
                state_proj[...],
                (((1,), (1,)), ((), ())),
                preferred_element_type=F32,
            )
        )
    local = jnp.concatenate(local, axis=0)
    piece = flat // n
    for k in range(n):
        part_proj[k] = local[k * piece : (k + 1) * piece].astype(BF16)
    pl.semaphore_wait(barrier, n - 1 + len(others))
    spread_out = {}
    for off in far_first(n):
        spread_out[off] = pltpu.make_async_remote_copy(
            src_ref=part_proj.at[lax.rem(me + off, n)],
            dst_ref=recv_proj.at[off],
            send_sem=sa.at[off],
            recv_sem=ra.at[off],
            device_id=along(off),
            device_id_type=MESH,
        )
        spread_out[off].start()

    def iota(shape, dim):
        return lax.broadcasted_iota(jnp.int32, shape, dim)

    rates[...] = -jnp.exp(decay_log[...])
    same_step = (iota((flat, flat), 0) // rows) == (iota((flat, flat), 1) // rows)
    upper = (same_step & (iota((flat, flat), 0) <= iota((flat, flat), 1))).astype(F32).astype(BF16)
    top = picked.shape[1]
    choice = [
        jnp.concatenate([picked[s, k : k + 1, :] for s in range(steps)], axis=1)
        for k in range(top)
    ]
    select = []
    for expert in range(row_size):
        hit = jnp.zeros((1, flat), F32)
        for k in range(top):
            hit = hit + (choice[k] == expert).astype(F32)
        count = jnp.dot(
            jnp.broadcast_to(hit, (slots, flat)).astype(BF16), upper, preferred_element_type=F32
        )
        slot = iota((slots, flat), 0)
        want = (slot % CAP + 1).astype(F32)
        ok = (slot // CAP == iota((slots, flat), 1) // rows) & (count == want)
        chosen = ok.astype(F32) * hit
        select.append(chosen.astype(BF16))
        for k in range(top):
            slot_id = jnp.sum(chosen * choice[k].astype(F32), axis=1, keepdims=True)
            id_stage[expert, :, k * LANES : (k + 1) * LANES] = jnp.broadcast_to(
                slot_id, (slots, LANES)
            ).astype(BF16)
    id_copies = []
    for a in range(1, row_size):
        copy = pltpu.make_async_remote_copy(
            src_ref=id_stage.at[lax.rem(row + a, row_size)],
            dst_ref=ids.at[row],
            send_sem=si.at[a],
            recv_sem=ri.at[a],
            device_id=at(a, 0),
            device_id_type=MESH,
        )
        copy.start()
        id_copies.append(copy)
    ids[row] = id_stage[row]

    total = part_proj[me].astype(F32)
    for off in reversed(far_first(n)):
        spread_out[off].wait_recv()
        total = total + recv_proj[off].astype(F32)
    own_proj[...] = total.astype(BF16)
    collect = {}
    for off in far_first(n):
        collect[off] = pltpu.make_async_remote_copy(
            src_ref=own_proj,
            dst_ref=full_proj.at[me],
            send_sem=sb.at[off],
            recv_sem=rb.at[off],
            device_id=along(off),
            device_id_type=MESH,
        )
        collect[off].start()
    full_proj[me] = own_proj[...]
    for off in reversed(far_first(n)):
        collect[off].wait_recv()
    summed = jnp.concatenate([full_proj[k].astype(F32) for k in range(n)], axis=0)
    raw = (
        jnp.dot(summed[:, :rank].astype(BF16), step_proj[...], preferred_element_type=F32)
        + step_bias[...]
    )
    soft = jnp.maximum(raw, 0.0) + jnp.log1p(jnp.exp(-jnp.abs(raw)))
    for s in range(steps):
        step_now = soft[s * rows : (s + 1) * rows]
        delta[s] = step_now
        moved[s] = step_now * convolved[s].astype(F32)
        for k in range(entries):
            column = summed[s * rows : (s + 1) * rows, rank + k : rank + k + 1]
            gain_in[s, :, k, :] = jnp.broadcast_to(column, (rows, LANES))
            column = summed[
                s * rows : (s + 1) * rows, rank + entries + k : rank + entries + k + 1
            ]
            gain_out[s, :, k, :] = jnp.broadcast_to(column, (rows, LANES))

    loads[4].wait()
    across = {}
    scanned = []
    for s in range(steps):

        def scan_rows(block, carry, s=s):
            start = pl.multiple_of(block * 8, 8)
            for c in range(0, inner, LANES):
                lane = slice(c, c + LANES)
                step_now = delta[s, pl.ds(start, 8), lane]
                moved_now = moved[s, pl.ds(start, 8), lane]
                lines = []
                for j in range(8):
                    held = (
                        jnp.exp(step_now[j : j + 1] * rates[:, lane]) * state[start + j, :, lane]
                        + moved_now[j : j + 1] * gain_in[s, start + j]
                    )
                    state[start + j, :, lane] = held
                    lines.append(
                        jnp.sum(gain_out[s, start + j] * held, axis=0, keepdims=True)
                    )
                readout[pl.ds(start, 8), lane] = jnp.concatenate(lines, axis=0)
            return carry

        lax.fori_loop(0, rows // 8, scan_rows, 0)
        result = readout[...] + skip_gain[...] * convolved[s].astype(F32)
        scanned.append((result * jax.nn.silu(xz[1, s].astype(F32))).astype(BF16))
        if s == 0:
            loads[0].wait()
        for off in order:
            to = lax.rem(place + off, pairs) * 2 + 1 - side
            cross1[s, off] = jnp.dot(
                scanned[s], out_weight[:, cols(to)], preferred_element_type=F32
            ).astype(BF16)
            across[s, off] = pltpu.make_async_remote_copy(
                src_ref=cross1.at[s, off],
                dst_ref=met1.at[s, off],
                send_sem=sc1.at[s, off],
                recv_sem=rc1.at[s, off],
                device_id=partner,
                device_id_type=MESH,
            )
            across[s, off].start()
    write_state = pltpu.make_async_copy(state, new_state, load_sem.at[5])
    write_state.start()
    first = {}
    totals = []
    for s in range(steps):
        for off in order:
            to = lax.rem(place + off, pairs) * 2 + side
            part = jnp.dot(scanned[s], out_weight[:, cols(to)], preferred_element_type=F32)
            across[s, off].wait_recv()
            part = part + met1[s, off].astype(F32)
            if off:
                send1[s, off] = part.astype(BF16)
                first[s, off] = pltpu.make_async_remote_copy(
                    src_ref=send1.at[s, off],
                    dst_ref=recv1.at[s, off],
                    send_sem=s1.at[s, off],
                    recv_sem=r1.at[s, off],
                    device_id=at(0, off),
                    device_id_type=MESH,
                )
                first[s, off].start()
            else:
                totals.append(stream[s].astype(F32) + part)
    for s in range(steps):
        for off in reversed(order[:-1]):
            first[s, off].wait_recv()
            totals[s] = totals[s] + recv1[s, off].astype(F32)
    after = jnp.concatenate(totals, axis=0).astype(BF16)

    for expert in range(row_size):
        stage[expert] = jnp.dot(select[expert], after, preferred_element_type=F32).astype(BF16)
    second = {}
    for a, b in reversed(peers):
        second[a, b] = pltpu.make_async_remote_copy(
            src_ref=stage.at[lax.rem(row + a, row_size)],
            dst_ref=gathered.at[row, me],
            send_sem=s2.at[a, b],
            recv_sem=r2.at[a, b],
            device_id=at(a, b),
            device_id_type=MESH,
        )
        second[a, b].start()
    gathered[row, me] = stage[row]
    onward = []
    for a, b in [(0, 0)] + peers:
        r = lax.rem(row - a + row_size, row_size)
        m = lax.rem(place - b + pairs, pairs) * 2 + side
        if a or b:
            second[a, b].wait_recv()
            block = gathered.at[r, m]
        else:
            block = stage.at[row]
        copy = pltpu.make_async_remote_copy(
            src_ref=block,
            dst_ref=gathered.at[r, m],
            send_sem=sf.at[a, b],
            recv_sem=rf.at[a, b],
            device_id=partner,
            device_id_type=MESH,
        )
        copy.start()
        onward.append(copy)
    for copy in onward:
        copy.wait_recv()
    for copy in id_copies:
        copy.wait_recv()
    for r in range(row_size):
        square = jnp.zeros((slots, 1), F32)
        for m in range(n):
            piece = gathered[r, m].astype(F32)
            square = square + jnp.sum(piece * piece, axis=1, keepdims=True)
        scale = lax.rsqrt(square / full + 1e-05)
        for m in range(n):
            piece = gathered[r, m].astype(F32)
            normed[r * slots : (r + 1) * slots, m * width : (m + 1) * width] = (
                piece * scale * gain[:, m * width : (m + 1) * width]
            ).astype(BF16)
    logits = lax.dot_general(
        normed[...], router[...], (((1,), (1,)), ((), ())), preferred_element_type=F32
    )
    slot_ids = jnp.concatenate([ids[r] for r in range(row_size)], axis=0).astype(F32)
    experts = logits.shape[1]
    column = iota(logits.shape, 1).astype(F32)
    mine = row.astype(F32)
    weight_sum = jnp.zeros((row_size * slots, 1), F32)
    weight_own = jnp.zeros((row_size * slots, 1), F32)
    for k in range(top):
        chosen_id = slot_ids[:, k * LANES : k * LANES + experts]
        chosen = jnp.sum(jnp.where(chosen_id == column, logits, 0.0), axis=1, keepdims=True)
        weight = jnp.exp(chosen)
        weight_sum = weight_sum + weight
        weight_own = weight_own + jnp.where(chosen_id[:, :1] == mine, weight, 0.0)
    share = weight_own / weight_sum

    loads[1].wait()
    loads[2].wait()

    def gate_up(i, carry):
        span = pl.ds(pl.multiple_of(i * tile, tile), tile)
        x = normed[...]
        g = jnp.dot(x, gate[:, span], preferred_element_type=F32)
        u = jnp.dot(x, up[:, span], preferred_element_type=F32)
        hidden[:, span] = (jax.nn.silu(g) * u).astype(BF16)
        return carry

    lax.fori_loop(0, gate.shape[1] // tile, gate_up, 0)
    loads[3].wait()
    back = {}
    for b in order:
        to = lax.rem(place + b, pairs) * 2 + 1 - side
        cross2[b] = (
            jnp.dot(hidden[...], down[:, cols(to)], preferred_element_type=F32) * share
        ).astype(BF16)
        back[b] = pltpu.make_async_remote_copy(
            src_ref=cross2.at[b],
            dst_ref=met2.at[b],
            send_sem=sc2.at[b],
            recv_sem=rc2.at[b],
            device_id=partner,
            device_id_type=MESH,
        )
        back[b].start()
    third = []
    for b in order:
        to = lax.rem(place + b, pairs) * 2 + side
        part = jnp.dot(hidden[...], down[:, cols(to)], preferred_element_type=F32) * share
        back[b].wait_recv()
        part = part + met2[b].astype(F32)
        for r in range(row_size):
            send2[b, r] = part[r * slots : (r + 1) * slots].astype(BF16)
        for a in range(row_size):
            if a or b:
                copy = pltpu.make_async_remote_copy(
                    src_ref=send2.at[b, lax.rem(row + a, row_size)],
                    dst_ref=recv2.at[row, b],
                    send_sem=s3.at[a, b],
                    recv_sem=r3.at[a, b],
                    device_id=at(a, b),
                    device_id_type=MESH,
                )
                copy.start()
                third.append(copy)
    recv2[row, 0] = send2[0, row]
    for copy in third:
        copy.wait_recv()
    combined = jnp.zeros((flat, width), F32)
    for expert in range(row_size):
        got = recv2[expert, 0].astype(F32)
        for b in range(1, pairs):
            got = got + recv2[expert, b].astype(F32)
        high = got.astype(BF16)
        low = (got - high.astype(F32)).astype(BF16)
        for piece_now in (high, low):
            combined = combined + lax.dot_general(
                select[expert],
                piece_now,
                (((0,), (0,)), ((), ())),
                preferred_element_type=F32,
            )
    mixed = after.astype(F32) + combined
    for s in range(steps):
        o_ref[s] = mixed[s * rows : (s + 1) * rows].astype(o_ref.dtype)
    sent = [spread_out, collect, across, first, second, back]
    for copy in id_copies + [c for group in sent for c in group.values()] + onward + third:
        copy.wait_send()
    write_state.wait()


def on_device(
    stream,
    projected,
    conv_state,
    scan_state,
    conv_weight,
    conv_bias,
    state_proj,
    step_proj,
    step_bias,
    decay_log,
    skip_gain,
    out_weight,
    norm_gain,
    router,
    expert_gate,
    expert_up,
    expert_down,
    expert_ids,
):
    n = lax.axis_size("mp")
    row_size = lax.axis_size("row")
    steps, rows, width = stream.shape
    inner = projected.shape[3]
    entries = decay_log.shape[0]
    columns = state_proj.shape[1]
    full = out_weight.shape[1]
    ff = expert_gate.shape[2]
    top = expert_ids.shape[2]
    flat = steps * rows
    slots = steps * CAP
    pairs = n // 2
    piece = flat // n
    tile = 256 if ff % 256 == 0 else 128
    dma = pltpu.SemaphoreType.DMA
    vmem = pl.BlockSpec(memory_space=pltpu.VMEM)
    hbm = pl.BlockSpec(memory_space=pl.ANY)

    def half(*shape):
        return pltpu.VMEM(shape, BF16)

    def wide(*shape):
        return pltpu.VMEM(shape, F32)

    return pl.pallas_call(
        functools.partial(kernel, n, row_size, tile),
        out_shape=(
            jax.ShapeDtypeStruct(stream.shape, stream.dtype),
            jax.ShapeDtypeStruct(scan_state.shape, scan_state.dtype),
        ),
        in_specs=[vmem] * 13 + [hbm] * 5,
        out_specs=(vmem, hbm),
        scratch_shapes=[
            wide(rows, entries, inner),
            half(steps, rows, inner),
            wide(steps, rows, inner),
            wide(steps, rows, inner),
            wide(rows, inner),
            wide(steps, rows, entries, LANES),
            wide(steps, rows, entries, LANES),
            wide(entries, inner),
            half(n, piece, columns),
            half(n, piece, columns),
            half(piece, columns),
            half(n, piece, columns),
            half(*out_weight.shape),
            half(*expert_gate.shape[1:]),
            half(*expert_up.shape[1:]),
            half(*expert_down.shape[1:]),
            half(steps, pairs, rows, width),
            half(steps, pairs, rows, width),
            half(row_size, slots, width),
            half(row_size, n, slots, width),
            half(row_size, slots, LANES * top),
            half(row_size, slots, LANES * top),
            half(row_size * slots, full),
            half(row_size * slots, ff),
            half(pairs, row_size, slots, width),
            half(row_size, pairs, slots, width),
            half(steps, pairs, rows, width),
            half(steps, pairs, rows, width),
            half(pairs, row_size * slots, width),
            half(pairs, row_size * slots, width),
            dma((6,)),
            dma((n,)),
            dma((n,)),
            dma((n,)),
            dma((n,)),
            dma((steps, pairs)),
            dma((steps, pairs)),
            dma((row_size, pairs)),
            dma((row_size, pairs)),
            dma((row_size,)),
            dma((row_size,)),
            dma((row_size, pairs)),
            dma((row_size, pairs)),
            dma((steps, pairs)),
            dma((steps, pairs)),
            dma((row_size, pairs)),
            dma((row_size, pairs)),
            dma((pairs,)),
            dma((pairs,)),
        ],
        compiler_params=pltpu.CompilerParams(
            collective_id=0, has_side_effects=True, vmem_limit_bytes=62 * 1024 * 1024
        ),
        name="decode",
    )(
        jnp.transpose(projected, (2, 0, 1, 3)),
        jnp.transpose(conv_state, (1, 0, 2)),
        conv_weight,
        conv_bias.reshape(1, -1),
        jnp.transpose(state_proj),
        step_proj,
        step_bias.reshape(1, -1),
        decay_log,
        skip_gain.reshape(1, -1),
        stream,
        norm_gain.reshape(1, -1),
        router,
        jnp.transpose(expert_ids, (0, 2, 1)),
        scan_state,
        out_weight,
        expert_gate,
        expert_up,
        expert_down,
    )


def solution(mesh):
    return jax.shard_map(
        on_device,
        mesh=mesh,
        in_specs=(
            P(None, ("groups", "row"), "mp"),
            P(None, ("groups", "row"), None, "mp"),
            P(("groups", "row"), None, "mp"),
            P(("groups", "row"), None, "mp"),
            P(None, "mp"),
            P("mp"),
            P("mp", None),
            P(None, "mp"),
            P("mp"),
            P(None, "mp"),
            P("mp"),
            P("mp", None),
            P(),
            P(),
            P("row", None, "mp"),
            P("row", None, "mp"),
            P("row", "mp", None),
            P(None, ("groups", "row"), None),
        ),
        out_specs=(P(None, ("groups", "row"), "mp"), P(("groups", "row"), None, "mp")),
        check_vma=False,
    )
```

time: 83.6 us -> 74.1 us (0.89)
  other arithmetic: 8.94 us -> 0 us
  local copies, waits for them, and re-layouts: 5.01 us -> 8.31 us
  matrix products: 1.85 us -> 0 us
  Pallas kernels: 66.7 us -> 64.9 us
    reduce_sum x2 -> x0, other arithmetic: 5.53 us -> none  [the longest x1 4.59 us: on_device(): jnp.sum(output_gain[step_no][:, :, None] * carried, axis=1)]
    unnamed x23 -> x3, local copies, waits for them, and re-layouts: 2.84 us -> 8.31 us
    dot_general x2 -> x0, matrix products: 1.85 us -> none  [the longest x1 1.53 us: on_device(): jnp.dot(low_rank.reshape(flat_rows, rank_size), step_proj, preferred_elem...]
    pallas_call x2 -> x1, Pallas kernels: 66.7 us -> 64.9 us  [on_device(): pl.pallas_call(functools.partial(kernel, n, row_size, tile), out_shape=(j...]
    convert_element_type x3 -> x0, other arithmetic: 1.39 us -> none  [the longest x1 1.01 us: on_device(): projections[..., rank_size:rank_size + state_size].astype(jnp.float32)]
    concatenate x1 -> x0, other arithmetic: 1.09 us -> none  [on_device(): jnp.concatenate([conv_state.astype(jnp.float32), jnp.transpose(inputs, (1...]
where the time goes in v3:
time: 74.1 us; the launch traced here: 73.8 us
  Pallas kernels  64.9 us (88%)
  local copies, waits for them, and re-layouts  8.31 us (11%)
    pallas_call x1, Pallas kernels, on_device(): pl.pallas_call(functools.partial(kernel, n, row_size, tile), out_shape=(j...  64.9 us
    unnamed x3, local copies, waits for them, and re-layouts  8.31 us

profile of v3, /device:TPU:0, one launch (start us, length us, event | category | flops | bytes accessed | tf_op | source)
XLA Modules:
  0.0 73.8 jit_solution(17521688555555942648)
XLA Ops:
  0.6 2.0 %copy.22 = bf16[2,64,2,1024]{3,1,0,2:T(8,128)(2,1)} copy(bf16[2,64,2,1024]{3,2,1,0:T(2,128)(2,1)} %param.19) | data formatting | bytes 1048576 | tf_op args[1]
  2.6 64.9 %decode.1 = (bf16[2,64,512]{2,1,0:T(8,128)(2,1)}, f32[64,16,1024]{2,1,0:T(8,128)}) custom-call(bf16[2,2,64,1024]{3,2,1,0:T(8,128)(2,1)} %bitcast.10, bf16[3,64,1024]{2,1,0:T(8,128)(2,1)} %bitcast.12, f32[4,1024]{1,0:T(4,128)} %conv_weight.1, f32[1,1024]{1,0:T(1,128)} %bitcast.14, bf16[288,1024]{1,0:T(8,128)(2,1)} %bitcast.11, bf16[256,1024]{1,0:T(8,128)(2,1)} %step_proj.1, ...), custom_call_target="tpu_custom_call" | custom-call | tf_op jit(solution)/shard_map/decode/pallas_call | solution.py:511
  67.5 1.6 %copy.25 = bf16[2,64,512]{2,1,0:T(8,128)(2,1)} copy(bf16[2,64,512]{2,1,0:T(8,128)(2,1)} %get-tuple-element.4) | data formatting | bytes 262144
  69.0 4.8 %copy.26 = f32[64,16,1024]{2,1,0:T(8,128)} copy(f32[64,16,1024]{2,1,0:T(8,128)} %get-tuple-element.5) | data formatting | bytes 8388608

commit v4 on v3

--- a/solution.py
+++ b/solution.py
@@ -41,7 +41,6 @@
     up_hbm,
     down_hbm,
     o_ref,
-    new_state,
     state,
     convolved,
     delta,
@@ -296,8 +295,6 @@
                 device_id_type=MESH,
             )
             across[s, off].start()
-    write_state = pltpu.make_async_copy(state, new_state, load_sem.at[5])
-    write_state.start()
     first = {}
     totals = []
     for s in range(steps):
@@ -461,7 +458,6 @@
     sent = [spread_out, collect, across, first, second, back]
     for copy in id_copies + [c for group in sent for c in group.values()] + onward + third:
         copy.wait_send()
-    write_state.wait()
 
 
 def on_device(
@@ -511,13 +507,12 @@
     return pl.pallas_call(
         functools.partial(kernel, n, row_size, tile),
         out_shape=(
-            jax.ShapeDtypeStruct(stream.shape, stream.dtype),
-            jax.ShapeDtypeStruct(scan_state.shape, scan_state.dtype),
+            half(*stream.shape),
+            wide(*scan_state.shape),
         ),
         in_specs=[vmem] * 13 + [hbm] * 5,
-        out_specs=(vmem, hbm),
+        out_specs=(vmem, vmem),
         scratch_shapes=[
-            wide(rows, entries, inner),
             half(steps, rows, inner),
             wide(steps, rows, inner),
             wide(steps, rows, inner),
@@ -547,7 +542,7 @@
             half(steps, pairs, rows, width),
             half(pairs, row_size * slots, width),
             half(pairs, row_size * slots, width),
-            dma((6,)),
+            dma((5,)),
             dma((n,)),
             dma((n,)),
             dma((n,)),
@@ -568,7 +563,7 @@
             dma((pairs,)),
         ],
         compiler_params=pltpu.CompilerParams(
-            collective_id=0, has_side_effects=True, vmem_limit_bytes=62 * 1024 * 1024
+            collective_id=0, has_side_effects=True, vmem_limit_bytes=57 * 1024 * 1024
         ),
         name="decode",
     )(

time: 74.1 us -> 69.6 us (0.939)
  local copies, waits for them, and re-layouts: 8.31 us -> 4.62 us
  Pallas kernels: 64.9 us -> 64.1 us
    unnamed x3, local copies, waits for them, and re-layouts: 8.31 us -> 4.62 us
where the time goes in v4:
time: 69.6 us; the launch traced here: 69.4 us
  Pallas kernels  64.1 us (92%)
  local copies, waits for them, and re-layouts  4.62 us (7%)
    pallas_call x1, Pallas kernels, on_device(): pl.pallas_call(functools.partial(kernel, n, row_size, tile), out_shape=(h...  64.1 us
    unnamed x3, local copies, waits for them, and re-layouts  4.62 us

profile of v4, /device:TPU:0, one launch (start us, length us, event | category | flops | bytes accessed | tf_op | source)
XLA Modules:
  0.0 69.4 jit_solution(15449925452327280348)
XLA Ops:
  0.6 2.0 %copy.22 = bf16[2,64,2,1024]{3,1,0,2:T(8,128)(2,1)} copy(bf16[2,64,2,1024]{3,2,1,0:T(2,128)(2,1)} %param.19) | data formatting | bytes 1048576 | tf_op args[1]
  2.6 64.1 %decode.1 = (bf16[2,64,512]{2,1,0:T(8,128)(2,1)S(1)}, f32[64,16,1024]{2,1,0:T(8,128)S(1)}) custom-call(bf16[2,2,64,1024]{3,2,1,0:T(8,128)(2,1)} %bitcast.10, bf16[3,64,1024]{2,1,0:T(8,128)(2,1)} %bitcast.12, f32[4,1024]{1,0:T(4,128)} %conv_weight.1, f32[1,1024]{1,0:T(1,128)} %bitcast.14, bf16[288,1024]{1,0:T(8,128)(2,1)} %bitcast.11, ...), custom_call_target="tpu_custom_call" | custom-call | tf_op jit(solution)/shard_map/decode/pallas_call | solution.py:507
  66.7 0.7 copy.25
  67.4 2.0 %copy.26 = f32[64,16,1024]{2,1,0:T(8,128)} copy(f32[64,16,1024]{2,1,0:T(8,128)S(1)} %get-tuple-element.3) | data formatting | bytes 8388608
